TPU v7x, 32 devices: a whole 2x2x4 slice. The times are simulated.
32 devices in a mesh: groups: 2 (over x), span: 16 (over z, y, core).
Axes of the slice: x: 2, y: 2, z: 4, core: 2. Of those that a mesh axis runs over, the one named last changes fastest.
Arguments:
- queries: bfloat16 [4096, 2560], P(('groups', 'span')), parts along dimension 0, may hold values from -6 to 6
- keys: bfloat16 [4096, 2560], P(('groups', 'span')), parts along dimension 0, may hold values from -6 to 6
- values: bfloat16 [4096, 2560], P(('groups', 'span')), parts along dimension 0, may hold values from -6 to 6
- lookback: int32 [32], P(('groups', 'span')), parts along dimension 0, may hold values from 0 to 3, as said below
- proj_weight: bfloat16 [2560, 768], replicated, may hold values from -0.125 to 0.125
- features: bfloat16 [64, 192, 256], P(('groups', 'span')), parts along dimension 0, may hold values from -0.29882812 to 0.29882812
- norm_gain: float32 [192], replicated, may hold values from 0.1 to 1.9
- conv_weight: bfloat16 [27, 192, 192], replicated, may hold values from -0.078125 to 0.078125
Outputs:
- attended: bfloat16 [4096, 2560], P(('groups', 'span')), parts along dimension 0
- decoded: bfloat16 [64, 192, 256], P(('groups', 'span')), parts along dimension 0
There are 2 independent parts, one for each index of `groups`. A program takes and returns all parts, laid end to end along the dimension named above; an argument that names none is the same for every part. Nothing has to cross between parts.
Inputs may be any that keep to these rules, and one draw needn't show every extreme that they name: lookback[c] <= c for every span c; the last span's value is 3.
All inputs are finite; a program needn't handle non-finite values.
Results may differ from a plain program's by a relative error of at most 0.0069.
Values may be sent and summed in bfloat16 or wider, within the bound.
A program may use at most 64 MiB of HBM per device.

v0:
```python
import functools

import jax
import jax.numpy as jnp
from jax import lax
from jax.experimental import pallas as pl
from jax.experimental.pallas import tpu as pltpu
from jax.sharding import PartitionSpec as P

HEAD_DIM = 128
LOOKBACK = 3
SIDE = 16
PLANE = SIDE * SIDE
HEADS_PER_CHUNK = 2
CHUNK = HEADS_PER_CHUNK * HEAD_DIM
AHEAD = 4
MESH = pl.DeviceIdType.MESH
F32 = jnp.float32
BF16 = jnp.bfloat16

eps = 1e-06

PARTNERS = ((1, 2, -3, -1), (2, 3, 4, -1, 1, -4), (1, -1, -2, -3), (3, -1, -2, 1))
OWN, NEAR, MID, FAR, TRANSIT = range(5)


def kernel(
    n_span,
    look_ref,
    gain_ref,
    q_hbm,
    k_hbm,
    v_hbm,
    w_hbm,
    feat_hbm,
    cw_hbm,
    attb,
    decb,
    kv,
    qbuf,
    wbuf,
    fbuf,
    cwbuf,
    pacc,
    turned,
    sel,
    gain_col,
    act,
    halo,
    acc,
    own_sem,
    in_sem,
    ssem,
    rsem,
    hs_sem,
    hr_sem,
):
    width = qbuf.shape[1]
    chunks = width // CHUNK
    frames, channels = fbuf.shape[0], fbuf.shape[1]
    me = lax.axis_index("span")
    role = lax.rem(me, 4)
    has_prev = me >= 4
    has_next = me < n_span - 4

    def cols(j):
        return pl.ds(pl.multiple_of(j * CHUNK, CHUNK), CHUNK)

    def own_load(j, which):
        src = (k_hbm, v_hbm)[which]
        return pltpu.make_async_copy(src.at[:, cols(j)], kv.at[OWN, j, which], own_sem.at[which, j])

    def start_loads(j, carry):
        own_load(j, 0).start()
        own_load(j, 1).start()
        return carry

    lax.fori_loop(0, chunks, start_loads, 0)
    loads = [
        pltpu.make_async_copy(src, dst, in_sem.at[i])
        for i, (src, dst) in enumerate(((q_hbm, qbuf), (w_hbm, wbuf), (feat_hbm, fbuf), (cw_hbm, cwbuf)))
    ]
    loads[0].start()

    barrier = pltpu.get_barrier_semaphore()
    for kind in range(4):
        for offset in PARTNERS[kind]:
            other = me + offset

            @pl.when((role == kind) & (other >= 0) & (other < n_span))
            def _(other=other):
                pl.semaphore_signal(barrier, inc=1, device_id={"span": other}, device_id_type=MESH)

    greeted = jnp.int32(0)
    for kind in range(4):
        for offset in PARTNERS[kind]:
            other = me + offset
            greeted += ((role == kind) & (other >= 0) & (other < n_span)).astype(jnp.int32)
    pl.semaphore_wait(barrier, greeted)

    def copy(flow, src, dst, j, offset):
        return pltpu.make_async_remote_copy(
            src_ref=kv.at[src, j],
            dst_ref=kv.at[dst, j],
            send_sem=ssem.at[flow, j],
            recv_sem=rsem.at[dst, j],
            device_id={"span": me + offset},
            device_id_type=MESH,
        )

    def arrived(slot, j, offset):
        copy(0, slot, slot, j, offset).wait_recv()

    a0, a1, b0, b1 = (role == kind for kind in range(4))

    own_flows = (
        (a0, 0, OWN, MID, 2),
        (a0, 1, OWN, NEAR, 1),
        (a1, 0, OWN, MID, 2),
        (a1 & has_next, 1, OWN, FAR, 3),
        (b0 & has_next, 0, OWN, TRANSIT, -1),
        (b0, 1, OWN, NEAR, 1),
        (b1 & has_next, 0, OWN, FAR, 3),
    )
    early_relays = (
        (a1 & has_next, 2, TRANSIT, FAR, 4),
        (b0 & has_prev, 2, FAR, NEAR, -2),
    )
    first_relays = (
        (b0, 3, MID, FAR, 1),
        (b1, 1, MID, NEAR, -1),
    )
    second_relays = (
        (a0 & has_prev, 2, NEAR, MID, 1),
        (a1 & has_prev, 3, FAR, MID, -1),
    )
    arrivals = (
        (a0 & has_prev, MID),
        (a0 & has_prev, FAR),
        (a1, NEAR),
        (a1 & has_prev, MID),
        (b0, NEAR),
        (b1, NEAR),
        (b1, FAR),
    )

    def send_own(j):
        own_load(j, 0).wait()
        own_load(j, 1).wait()
        for cond, flow, src, dst, offset in own_flows:

            @pl.when(cond)
            def _(flow=flow, src=src, dst=dst, offset=offset):
                copy(flow, src, dst, j, offset).start()

    def pass_on(relays, j):
        for cond, flow, src, dst, offset in relays:

            @pl.when(cond)
            def _(flow=flow, src=src, dst=dst, offset=offset):
                arrived(src, j, offset)
                copy(flow, src, dst, j, offset).start()

    for j in range(AHEAD):
        send_own(jnp.int32(j))
    for load in loads[1:]:
        load.start()

    for distance in range(1, LOOKBACK + 1):

        @pl.when(me < distance)
        def _(distance=distance):
            kv[distance] = jnp.zeros(kv.shape[1:], BF16)

    pacc[...] = jnp.zeros_like(pacc)
    acc[...] = jnp.zeros_like(acc)
    rows = lax.broadcasted_iota(jnp.int32, sel.shape, 0)
    places = lax.broadcasted_iota(jnp.int32, sel.shape, 1)
    pixel = places & (PLANE - 1)
    token = (places >> 8) * (PLANE // 4) + (pixel >> 5) * (SIDE // 2) + ((pixel & (SIDE - 1)) >> 1)
    corner = ((pixel >> 4) & 1) * 2 + (pixel & 1)
    hit = ((rows & 127) == token) & ((rows >> 7) == corner)
    sel[...] = jnp.where(hit, 1.0, 0.0).astype(BF16)
    square = (channels, channels)
    diagonal = lax.broadcasted_iota(jnp.int32, square, 0) == lax.broadcasted_iota(jnp.int32, square, 1)
    gain_col[...] = jnp.sum(jnp.where(diagonal, gain_ref[...], 0.0), axis=1, keepdims=True)
    distance = lax.broadcasted_iota(jnp.int32, (1, (LOOKBACK + 1) * 128), 1) >> 7
    usable = distance <= look_ref[0]

    def attend(j):
        for cond, slot in arrivals:

            @pl.when(cond)
            def _(slot=slot):
                arrived(slot, j, 0)

        for head in range(HEADS_PER_CHUNK):
            at = pl.ds(pl.multiple_of(j * CHUNK + head * HEAD_DIM, HEAD_DIM), HEAD_DIM)
            within = slice(head * HEAD_DIM, (head + 1) * HEAD_DIM)
            keys = kv[0:4, j, 0, :, within].reshape(-1, HEAD_DIM)
            values = kv[0:4, j, 1, :, within].reshape(-1, HEAD_DIM)
            scores = lax.dot_general(
                qbuf[:, at], keys, (((1,), (1,)), ((), ())), preferred_element_type=F32
            ) * HEAD_DIM ** (-0.5)
            scores = jnp.where(usable, scores, -jnp.inf)
            row_max = jnp.max(scores, axis=1, keepdims=True)
            weights = jnp.exp(scores - row_max)
            row_total = jnp.sum(weights, axis=1, keepdims=True)
            blended = jnp.dot(weights.astype(BF16), values, preferred_element_type=F32)
            attb[:, at] = (blended / row_total).astype(BF16)
        pacc[...] += jnp.dot(attb[:, cols(j)], wbuf[cols(j), :], preferred_element_type=F32)

    pass_on(early_relays, jnp.int32(0))

    def turn(i, carry):
        @pl.when(i + AHEAD < chunks)
        def _():
            send_own(i + AHEAD)

        @pl.when(i + 1 < chunks)
        def _():
            pass_on(early_relays, i + 1)

        @pl.when(i < chunks)
        def _():
            pass_on(first_relays, i)

        @pl.when((i >= 1) & (i < chunks + 1))
        def _():
            pass_on(second_relays, i - 1)

        @pl.when(i == 2)
        def _():
            loads[0].wait()
            loads[1].wait()

        @pl.when(i >= 2)
        def _():
            attend(i - 2)

        return carry

    lax.fori_loop(0, chunks + 2, turn, 0)

    loads[2].wait()
    loads[3].wait()
    turned[...] = pacc[...].T
    corners = [turned[pl.ds(corner, channels, stride=4), :] for corner in range(4)]
    tall = jnp.concatenate(corners, axis=1)
    high = tall.astype(BF16)
    low = (tall - high.astype(F32)).astype(BF16)
    spread = jnp.dot(high, sel[...], preferred_element_type=F32) + jnp.dot(low, sel[...], preferred_element_type=F32)

    def halo_copy(frame):
        return pltpu.make_async_remote_copy(
            src_ref=act.at[frame],
            dst_ref=halo.at[frame],
            send_sem=hs_sem.at[frame],
            recv_sem=hr_sem.at[frame],
            device_id={"span": me + 1},
            device_id_type=MESH,
        )

    for frame in range(frames):
        latent = (fbuf[frame].astype(F32) + spread[:, frame * PLANE : (frame + 1) * PLANE]).astype(BF16)
        decb[frame] = latent
        data = latent.astype(F32)
        mean_square = jnp.mean(data * data, axis=0, keepdims=True)
        normed = data * lax.rsqrt(mean_square + eps) * gain_col[...]
        act[frame] = (normed / (1.0 + jnp.exp(-normed))).astype(BF16)

        @pl.when(me < n_span - 1)
        def _(frame=frame):
            halo_copy(frame).start()

    lane = lax.broadcasted_iota(jnp.int32, (1, PLANE), 1)
    line, column = lane >> 4, lane & (SIDE - 1)

    def shifted(data, lag_y, lag_x):
        offset = (lag_y - 1) * SIDE + lag_x - 1
        window = data if offset == 0 else pltpu.roll(data, (-offset) % PLANE, 1)
        to_y, to_x = line + (lag_y - 1), column + (lag_x - 1)
        inside = (to_y >= 0) & (to_y < SIDE) & (to_x >= 0) & (to_x < SIDE)
        return jnp.where(inside, window, 0.0).astype(BF16)

    def tap(lag_t, place, window):
        return jnp.dot(cwbuf[lag_t * 9 + place], window, preferred_element_type=F32)

    first, second = act[0].astype(F32), act[1].astype(F32)
    for place in range(9):
        w0, w1 = (shifted(data, place // 3, place % 3) for data in (first, second))
        acc[0] += tap(2, place, w0)
        acc[1] += tap(1, place, w0) + tap(2, place, w1)

    @pl.when(me > 0)
    def _():
        halo_copy(0).wait_recv()
        halo_copy(1).wait_recv()
        before, last = halo[0].astype(F32), halo[1].astype(F32)
        for place in range(9):
            w0, w1 = (shifted(data, place // 3, place % 3) for data in (before, last))
            acc[0] += tap(0, place, w0) + tap(1, place, w1)
            acc[1] += tap(0, place, w1)

    for frame in range(frames):
        decb[frame] = (decb[frame].astype(F32) + acc[frame]).astype(BF16)

    @pl.when(me < n_span - 1)
    def _():
        halo_copy(0).wait_send()
        halo_copy(1).wait_send()

    def finish(j, carry):
        for cond, flow, src, dst, offset in own_flows + early_relays + first_relays + second_relays:

            @pl.when(cond)
            def _(flow=flow, src=src, dst=dst, offset=offset):
                copy(flow, src, dst, j, offset).wait_send()

        return carry

    lax.fori_loop(0, chunks, finish, 0)


def publish(att_vmem, dec_vmem, att_hbm, dec_hbm, sem):
    copies = [
        pltpu.make_async_copy(src, dst, sem.at[i])
        for i, (src, dst) in enumerate(((att_vmem, att_hbm), (dec_vmem, dec_hbm)))
    ]
    for copy in copies:
        copy.start()
    for copy in copies:
        copy.wait()


def solution(mesh):
    n_span = mesh.shape["span"]

    def shards(queries, keys, values, lookback, proj_weight, features, norm_gain, conv_weight):
        tokens, width = queries.shape
        frames, channels, plane = features.shape
        chunks = width // CHUNK
        patch = proj_weight.shape[1]
        dma = pltpu.SemaphoreType.DMA
        hbm = pl.BlockSpec(memory_space=pltpu.HBM)
        vmem = pl.BlockSpec(memory_space=pltpu.VMEM)
        attended, decoded = pl.pallas_call(
            functools.partial(kernel, n_span),
            out_shape=(
                pltpu.VMEM(queries.shape, BF16),
                pltpu.VMEM(features.shape, BF16),
            ),
            in_specs=[
                pl.BlockSpec(memory_space=pltpu.SMEM),
                pl.BlockSpec(memory_space=pltpu.VMEM),
            ]
            + [hbm] * 6,
            out_specs=(vmem, vmem),
            scratch_shapes=[
                pltpu.VMEM((5, chunks, 2, tokens, CHUNK), BF16),
                pltpu.VMEM((tokens, width), BF16),
                pltpu.VMEM(proj_weight.shape, BF16),
                pltpu.VMEM(features.shape, BF16),
                pltpu.VMEM(conv_weight.shape, BF16),
                pltpu.VMEM((tokens, patch), F32),
                pltpu.VMEM((patch, tokens), F32),
                pltpu.VMEM((4 * tokens, frames * plane), BF16),
                pltpu.VMEM((channels, 1), F32),
                pltpu.VMEM(features.shape, BF16),
                pltpu.VMEM(features.shape, BF16),
                pltpu.VMEM(features.shape, F32),
                dma((2, chunks)),
                dma((4,)),
                dma((4, chunks)),
                dma((5, chunks)),
                dma((2,)),
                dma((2,)),
            ],
            compiler_params=pltpu.CompilerParams(collective_id=0, has_side_effects=True),
        )(lookback, norm_gain.reshape(1, -1), queries, keys, values, proj_weight, features, conv_weight)
        return pl.pallas_call(
            publish,
            out_shape=(
                jax.ShapeDtypeStruct(queries.shape, BF16),
                jax.ShapeDtypeStruct(features.shape, BF16),
            ),
            in_specs=[vmem, vmem],
            out_specs=(hbm, hbm),
            scratch_shapes=[dma((2,))],
        )(
            pltpu.with_memory_space_constraint(attended, pltpu.VMEM),
            pltpu.with_memory_space_constraint(decoded, pltpu.VMEM),
        )

    rows = P(("groups", "span"), None)
    planes = P(("groups", "span"), None, None)
    return jax.shard_map(
        shards,
        mesh=mesh,
        in_specs=(rows, rows, rows, P(("groups", "span")), P(), planes, P(), P()),
        out_specs=(rows, planes),
        check_vma=False,
    )
```

profile of v0, /device:TPU:20, one launch (start us, length us, event | category | flops | bytes accessed | tf_op | source)
XLA Modules:
  0.0 43.5 jit_solution(15148031248058169052)
XLA Ops:
  1.3 41.3 %shard_map.95 = (bf16[128,2560]{1,0:T(8,128)(2,1)S(1)}, bf16[2,192,256]{2,1,0:T(8,128)(2,1)S(1)}) custom-call(s32[1]{0:T(128)S(6)} %copy.10.look_ref, f32[1,192]{1,0:T(1,128)} %bitcast.1, bf16[128,2560]{1,0:T(8,128)(2,1)} %q_hbm.1, bf16[128,2560]{1,0:T(8,128)(2,1)} %k_hbm.1, bf16[128,2560]{1,0:T(8,128)(2,1)} %v_hbm.1, bf16[2560,768]{1,0:T(8,128)(2,1)} %w_hbm.1, ...), custom_call_target="tpu_custom_call" | custom-call | tf_op jit(solution)/shard_map/pallas_call | solution.py:347
  42.6 0.9 %shard_map.96 = (bf16[128,2560]{1,0:T(8,128)(2,1)}, bf16[2,192,256]{2,1,0:T(8,128)(2,1)}) custom-call(bf16[128,2560]{1,0:T(8,128)(2,1)S(1)} %get-tuple-element.4.att_vmem, bf16[2,192,256]{2,1,0:T(8,128)(2,1)S(1)} %get-tuple-element.5.dec_vmem), custom_call_target="tpu_custom_call" | custom-call | tf_op jit(solution)/shard_map/pallas_call | solution.py:381
where the time goes:
time: 44.3 us; the launch traced here: 43.5 us
  Pallas kernels  42.2 us (95%)
  between operations  1.29 us (3%)
    pallas_call x1, Pallas kernels, shards(): pl.pallas_call(functools.partial(kernel, n_span), out_shape=(pltpu.VMEM(q...  41.3 us
    pallas_call x1, Pallas kernels, shards(): pl.pallas_call(publish, out_shape=(jax.ShapeDtypeStruct(queries.shape, BF...  0.91 us

commit v1 on v0

--- a/solution.py
+++ b/solution.py
@@ -48,6 +48,8 @@
     act,
     halo,
     acc,
+    wcat,
+    col,
     own_sem,
     in_sem,
     ssem,
@@ -102,7 +104,7 @@
         return pltpu.make_async_remote_copy(
             src_ref=kv.at[src, j],
             dst_ref=kv.at[dst, j],
-            send_sem=ssem.at[flow, j],
+            send_sem=ssem.at[flow],
             recv_sem=rsem.at[dst, j],
             device_id={"span": me + offset},
             device_id_type=MESH,
@@ -173,7 +175,6 @@
             kv[distance] = jnp.zeros(kv.shape[1:], BF16)
 
     pacc[...] = jnp.zeros_like(pacc)
-    acc[...] = jnp.zeros_like(acc)
     rows = lax.broadcasted_iota(jnp.int32, sel.shape, 0)
     places = lax.broadcasted_iota(jnp.int32, sel.shape, 1)
     pixel = places & (PLANE - 1)
@@ -221,29 +222,36 @@
         def _():
             pass_on(early_relays, i + 1)
 
-        @pl.when(i < chunks)
-        def _():
-            pass_on(first_relays, i)
-
-        @pl.when((i >= 1) & (i < chunks + 1))
-        def _():
-            pass_on(second_relays, i - 1)
-
-        @pl.when(i == 2)
+        @pl.when(i == 1)
         def _():
             loads[0].wait()
             loads[1].wait()
 
-        @pl.when(i >= 2)
-        def _():
-            attend(i - 2)
+        @pl.when(i == 2)
+        def _():
+            loads[3].wait()
+
+        for lag in range(3):
+
+            @pl.when(i == 3 + lag)
+            def _(lag=lag):
+                at = slice((2 - lag) * channels, (3 - lag) * channels)
+                wcat[at, :] = jnp.concatenate([cwbuf[lag * 9 + place] for place in range(9)], axis=1)
+
+        @pl.when(i >= 1)
+        def _():
+            attend(i - 1)
+
+        @pl.when(i < chunks)
+        def _():
+            pass_on(first_relays, i)
+            pass_on(second_relays, i)
 
         return carry
 
-    lax.fori_loop(0, chunks + 2, turn, 0)
+    lax.fori_loop(0, chunks + 1, turn, 0)
 
     loads[2].wait()
-    loads[3].wait()
     turned[...] = pacc[...].T
     corners = [turned[pl.ds(corner, channels, stride=4), :] for corner in range(4)]
     tall = jnp.concatenate(corners, axis=1)
@@ -276,31 +284,45 @@
     lane = lax.broadcasted_iota(jnp.int32, (1, PLANE), 1)
     line, column = lane >> 4, lane & (SIDE - 1)
 
-    def shifted(data, lag_y, lag_x):
-        offset = (lag_y - 1) * SIDE + lag_x - 1
-        window = data if offset == 0 else pltpu.roll(data, (-offset) % PLANE, 1)
-        to_y, to_x = line + (lag_y - 1), column + (lag_x - 1)
-        inside = (to_y >= 0) & (to_y < SIDE) & (to_x >= 0) & (to_x < SIDE)
-        return jnp.where(inside, window, 0.0).astype(BF16)
-
-    def tap(lag_t, place, window):
-        return jnp.dot(cwbuf[lag_t * 9 + place], window, preferred_element_type=F32)
-
-    first, second = act[0].astype(F32), act[1].astype(F32)
-    for place in range(9):
-        w0, w1 = (shifted(data, place // 3, place % 3) for data in (first, second))
-        acc[0] += tap(2, place, w0)
-        acc[1] += tap(1, place, w0) + tap(2, place, w1)
+    def keep(cond):
+        return jnp.where(cond, 1.0, 0.0).astype(BF16)
+
+    sides = (keep(column >= 1), None, keep(column < SIDE - 1))
+    ends = (keep(line >= 1), None, keep(line < SIDE - 1))
+
+    def shifted(data, shift, mask):
+        return data if mask is None else pltpu.roll(data, shift % PLANE, 1) * mask
+
+    def unfold(slot, data):
+        for lag_x in range(3):
+            across = shifted(data, 1 - lag_x, sides[lag_x])
+            for lag_y in range(3):
+                place = lag_y * 3 + lag_x
+                col[slot, place * channels : (place + 1) * channels, :] = shifted(
+                    across, (1 - lag_y) * SIDE, ends[lag_y]
+                )
+
+    def taps(slot, first, last):
+        return jnp.dot(
+            wcat[first * channels : last * channels, :], col[slot], preferred_element_type=F32
+        )
+
+    unfold(0, act[0])
+    both = taps(0, 0, 2)
+    acc[0] = both[:channels]
+    unfold(1, act[1])
+    acc[1] = both[channels:] + taps(1, 0, 1)
 
     @pl.when(me > 0)
     def _():
         halo_copy(0).wait_recv()
+        unfold(0, halo[0])
+        acc[0] += taps(0, 2, 3)
         halo_copy(1).wait_recv()
-        before, last = halo[0].astype(F32), halo[1].astype(F32)
-        for place in range(9):
-            w0, w1 = (shifted(data, place // 3, place % 3) for data in (before, last))
-            acc[0] += tap(0, place, w0) + tap(1, place, w1)
-            acc[1] += tap(0, place, w1)
+        unfold(1, halo[1])
+        both = taps(1, 1, 3)
+        acc[0] += both[:channels]
+        acc[1] += both[channels:]
 
     for frame in range(frames):
         decb[frame] = (decb[frame].astype(F32) + acc[frame]).astype(BF16)
@@ -310,16 +332,18 @@
         halo_copy(0).wait_send()
         halo_copy(1).wait_send()
 
-    def finish(j, carry):
-        for cond, flow, src, dst, offset in own_flows + early_relays + first_relays + second_relays:
-
-            @pl.when(cond)
-            def _(flow=flow, src=src, dst=dst, offset=offset):
-                copy(flow, src, dst, j, offset).wait_send()
-
-        return carry
-
-    lax.fori_loop(0, chunks, finish, 0)
+    for cond, flow, src, dst, offset in own_flows + early_relays + first_relays + second_relays:
+
+        @pl.when(cond)
+        def _(flow=flow, src=src, dst=dst, offset=offset):
+            pltpu.make_async_remote_copy(
+                src_ref=kv.at[src],
+                dst_ref=kv.at[dst],
+                send_sem=ssem.at[flow],
+                recv_sem=rsem.at[dst, 0],
+                device_id={"span": me + offset},
+                device_id_type=MESH,
+            ).wait_send()
 
 
 def publish(att_vmem, dec_vmem, att_hbm, dec_hbm, sem):
@@ -369,9 +393,11 @@
                 pltpu.VMEM(features.shape, BF16),
                 pltpu.VMEM(features.shape, BF16),
                 pltpu.VMEM(features.shape, F32),
+                pltpu.VMEM((3 * channels, 9 * channels), BF16),
+                pltpu.VMEM((2, 9 * channels, plane), BF16),
                 dma((2, chunks)),
                 dma((4,)),
-                dma((4, chunks)),
+                dma((4,)),
                 dma((5, chunks)),
                 dma((2,)),
                 dma((2,)),

time: 44.3 us -> 44.1 us (level); the launches traced: 43.5 us -> 43.9 us
  Pallas kernels: 42.2 us -> 42.7 us
    pallas_call x1, Pallas kernels: 41.3 us -> 41.8 us  [shards(): pl.pallas_call(functools.partial(kernel, n_span), out_shape=(pltpu.VMEM(q...]
where the time goes in v1:
time: 44.1 us; the launch traced here: 43.9 us
  Pallas kernels  42.7 us (97%)
  between operations  1.29 us (3%)
    pallas_call x1, Pallas kernels, shards(): pl.pallas_call(functools.partial(kernel, n_span), out_shape=(pltpu.VMEM(q...  41.8 us
    pallas_call x1, Pallas kernels, shards(): pl.pallas_call(publish, out_shape=(jax.ShapeDtypeStruct(queries.shape, BF...  0.91 us

profile of v1, /device:TPU:20, one launch (start us, length us, event | category | flops | bytes accessed | tf_op | source)
XLA Modules:
  0.0 43.9 jit_solution(10129899439306267487)
XLA Ops:
  1.3 41.8 %shard_map.95 = (bf16[128,2560]{1,0:T(8,128)(2,1)S(1)}, bf16[2,192,256]{2,1,0:T(8,128)(2,1)S(1)}) custom-call(s32[1]{0:T(128)S(6)} %copy.10.look_ref, f32[1,192]{1,0:T(1,128)} %bitcast.1, bf16[128,2560]{1,0:T(8,128)(2,1)} %q_hbm.1, bf16[128,2560]{1,0:T(8,128)(2,1)} %k_hbm.1, bf16[128,2560]{1,0:T(8,128)(2,1)} %v_hbm.1, bf16[2560,768]{1,0:T(8,128)(2,1)} %w_hbm.1, ...), custom_call_target="tpu_custom_call" | custom-call | tf_op jit(solution)/shard_map/pallas_call | solution.py:371
  43.0 0.9 %shard_map.96 = (bf16[128,2560]{1,0:T(8,128)(2,1)}, bf16[2,192,256]{2,1,0:T(8,128)(2,1)}) custom-call(bf16[128,2560]{1,0:T(8,128)(2,1)S(1)} %get-tuple-element.4.att_vmem, bf16[2,192,256]{2,1,0:T(8,128)(2,1)S(1)} %get-tuple-element.5.dec_vmem), custom_call_target="tpu_custom_call" | custom-call | tf_op jit(solution)/shard_map/pallas_call | solution.py:407

commit v2 on v1

--- a/solution.py
+++ b/solution.py
@@ -14,20 +14,21 @@
 HEADS_PER_CHUNK = 2
 CHUNK = HEADS_PER_CHUNK * HEAD_DIM
 AHEAD = 4
+LOWER = 8
 MESH = pl.DeviceIdType.MESH
 F32 = jnp.float32
 BF16 = jnp.bfloat16
 
 eps = 1e-06
 
-PARTNERS = ((1, 2, -3, -1), (2, 3, 4, -1, 1, -4), (1, -1, -2, -3), (3, -1, -2, 1))
+PARTNERS = ((1, 2, -3, -1), (2, 3, 4, -1, 1, -4), (1, -1, -2, -3, 4, -4), (3, -1, -2, 1))
 OWN, NEAR, MID, FAR, TRANSIT = range(5)
 
 
 def kernel(
     n_span,
-    look_ref,
-    gain_ref,
+    look_hbm,
+    gain_hbm,
     q_hbm,
     k_hbm,
     v_hbm,
@@ -50,6 +51,9 @@
     acc,
     wcat,
     col,
+    look_ref,
+    gain_ref,
+    part_sem,
     own_sem,
     in_sem,
     ssem,
@@ -60,11 +64,21 @@
     width = qbuf.shape[1]
     chunks = width // CHUNK
     frames, channels = fbuf.shape[0], fbuf.shape[1]
+    n_rows = n_span // 4
     me = lax.axis_index("span")
     role = lax.rem(me, 4)
     has_prev = me >= 4
     has_next = me < n_span - 4
 
+    barrier = pltpu.get_barrier_semaphore()
+    for kind in range(4):
+        for offset in PARTNERS[kind]:
+            other = me + offset
+
+            @pl.when((role == kind) & (other >= 0) & (other < n_span))
+            def _(other=other):
+                pl.semaphore_signal(barrier, inc=1, device_id={"span": other}, device_id_type=MESH)
+
     def cols(j):
         return pl.ds(pl.multiple_of(j * CHUNK, CHUNK), CHUNK)
 
@@ -80,18 +94,19 @@
     lax.fori_loop(0, chunks, start_loads, 0)
     loads = [
         pltpu.make_async_copy(src, dst, in_sem.at[i])
-        for i, (src, dst) in enumerate(((q_hbm, qbuf), (w_hbm, wbuf), (feat_hbm, fbuf), (cw_hbm, cwbuf)))
+        for i, (src, dst) in enumerate(
+            (
+                (q_hbm, qbuf),
+                (w_hbm, wbuf),
+                (feat_hbm, fbuf),
+                (cw_hbm, cwbuf),
+                (look_hbm, look_ref),
+                (gain_hbm, gain_ref),
+            )
+        )
     ]
-    loads[0].start()
-
-    barrier = pltpu.get_barrier_semaphore()
-    for kind in range(4):
-        for offset in PARTNERS[kind]:
-            other = me + offset
-
-            @pl.when((role == kind) & (other >= 0) & (other < n_span))
-            def _(other=other):
-                pl.semaphore_signal(barrier, inc=1, device_id={"span": other}, device_id_type=MESH)
+    for load in loads[4:] + loads[:1]:
+        load.start()
 
     greeted = jnp.int32(0)
     for kind in range(4):
@@ -114,18 +129,40 @@
         copy(0, slot, slot, j, offset).wait_recv()
 
     a0, a1, b0, b1 = (role == kind for kind in range(4))
+    row = me // 4
+
+    def crosses_below(row, j):
+        share = (LOWER * chunks * (n_rows - row)) // (10 * n_rows)
+        return ((j + 1) * share) // chunks > (j * share) // chunks
+
+    def part_flows(j):
+        here, before = crosses_below(row, j), crosses_below(row - 1, j)
+        return (
+            (b0 & has_next & here, 0, OWN, TRANSIT, -1),
+            (b0 & has_next & jnp.logical_not(here), 0, OWN, TRANSIT, 4),
+            (a1 & has_next & here, 0, TRANSIT, FAR, 4),
+            (b0 & has_prev & jnp.logical_not(before), 1, TRANSIT, FAR, -1),
+        )
+
+    def part_copy(flow, src, dst, j, offset):
+        return pltpu.make_async_remote_copy(
+            src_ref=kv.at[src, j],
+            dst_ref=kv.at[dst, j],
+            send_sem=part_sem.at[flow, j],
+            recv_sem=rsem.at[dst, j],
+            device_id={"span": me + offset},
+            device_id_type=MESH,
+        )
 
     own_flows = (
         (a0, 0, OWN, MID, 2),
         (a0, 1, OWN, NEAR, 1),
         (a1, 0, OWN, MID, 2),
         (a1 & has_next, 1, OWN, FAR, 3),
-        (b0 & has_next, 0, OWN, TRANSIT, -1),
         (b0, 1, OWN, NEAR, 1),
         (b1 & has_next, 0, OWN, FAR, 3),
     )
     early_relays = (
-        (a1 & has_next, 2, TRANSIT, FAR, 4),
         (b0 & has_prev, 2, FAR, NEAR, -2),
     )
     first_relays = (
@@ -155,6 +192,20 @@
             def _(flow=flow, src=src, dst=dst, offset=offset):
                 copy(flow, src, dst, j, offset).start()
 
+        for cond, flow, src, dst, offset in part_flows(j)[:2]:
+
+            @pl.when(cond)
+            def _(flow=flow, src=src, dst=dst, offset=offset):
+                part_copy(flow, src, dst, j, offset).start()
+
+    def pass_part(j):
+        for cond, flow, src, dst, offset in part_flows(j)[2:]:
+
+            @pl.when(cond)
+            def _(flow=flow, src=src, dst=dst, offset=offset):
+                arrived(src, j, offset)
+                part_copy(flow, src, dst, j, offset).start()
+
     def pass_on(relays, j):
         for cond, flow, src, dst, offset in relays:
 
@@ -165,7 +216,7 @@
 
     for j in range(AHEAD):
         send_own(jnp.int32(j))
-    for load in loads[1:]:
+    for load in loads[1:4]:
         load.start()
 
     for distance in range(1, LOOKBACK + 1):
@@ -184,6 +235,8 @@
     sel[...] = jnp.where(hit, 1.0, 0.0).astype(BF16)
     square = (channels, channels)
     diagonal = lax.broadcasted_iota(jnp.int32, square, 0) == lax.broadcasted_iota(jnp.int32, square, 1)
+    for load in loads[4:]:
+        load.wait()
     gain_col[...] = jnp.sum(jnp.where(diagonal, gain_ref[...], 0.0), axis=1, keepdims=True)
     distance = lax.broadcasted_iota(jnp.int32, (1, (LOOKBACK + 1) * 128), 1) >> 7
     usable = distance <= look_ref[0]
@@ -211,6 +264,7 @@
             attb[:, at] = (blended / row_total).astype(BF16)
         pacc[...] += jnp.dot(attb[:, cols(j)], wbuf[cols(j), :], preferred_element_type=F32)
 
+    pass_part(jnp.int32(0))
     pass_on(early_relays, jnp.int32(0))
 
     def turn(i, carry):
@@ -220,6 +274,7 @@
 
         @pl.when(i + 1 < chunks)
         def _():
+            pass_part(i + 1)
             pass_on(early_relays, i + 1)
 
         @pl.when(i == 1)
@@ -331,6 +386,19 @@
     def _():
         halo_copy(0).wait_send()
         halo_copy(1).wait_send()
+
+    def finish(j, carry):
+        for cond, flow, src, dst, offset in part_flows(j):
+
+            @pl.when(cond)
+            def _(flow=flow, src=src, dst=dst, offset=offset):
+                part_copy(flow, src, dst, j, offset).wait_send()
+
+        return carry
+
+    @pl.when(a1 | b0)
+    def _():
+        lax.fori_loop(0, chunks, finish, 0)
 
     for cond, flow, src, dst, offset in own_flows + early_relays + first_relays + second_relays:
 
@@ -374,11 +442,7 @@
                 pltpu.VMEM(queries.shape, BF16),
                 pltpu.VMEM(features.shape, BF16),
             ),
-            in_specs=[
-                pl.BlockSpec(memory_space=pltpu.SMEM),
-                pl.BlockSpec(memory_space=pltpu.VMEM),
-            ]
-            + [hbm] * 6,
+            in_specs=[hbm] * 8,
             out_specs=(vmem, vmem),
             scratch_shapes=[
                 pltpu.VMEM((5, chunks, 2, tokens, CHUNK), BF16),
@@ -395,8 +459,11 @@
                 pltpu.VMEM(features.shape, F32),
                 pltpu.VMEM((3 * channels, 9 * channels), BF16),
                 pltpu.VMEM((2, 9 * channels, plane), BF16),
+                pltpu.SMEM((1,), jnp.int32),
+                pltpu.VMEM((1, channels), F32),
                 dma((2, chunks)),
-                dma((4,)),
+                dma((2, chunks)),
+                dma((6,)),
                 dma((4,)),
                 dma((5, chunks)),
                 dma((2,)),

time: 44.1 us -> 45.5 us (1.032)
  Pallas kernels: 42.7 us -> 44 us
    pallas_call x1, Pallas kernels: 41.8 us -> 43.1 us  [shards(): pl.pallas_call(functools.partial(kernel, n_span), out_shape=(pltpu.VMEM(q...]
where the time goes in v2:
time: 45.5 us; the launch traced here: 45.3 us
  Pallas kernels  44 us (97%)
  between operations  1.29 us (3%)
    pallas_call x1, Pallas kernels, shards(): pl.pallas_call(functools.partial(kernel, n_span), out_shape=(pltpu.VMEM(q...  43.1 us
    pallas_call x1, Pallas kernels, shards(): pl.pallas_call(publish, out_shape=(jax.ShapeDtypeStruct(queries.shape, BF...  0.91 us

profile of v2, /device:TPU:20, one launch (start us, length us, event | category | flops | bytes accessed | tf_op | source)
XLA Modules:
  0.0 45.3 jit_solution(4937051689478408758)
XLA Ops:
  1.3 43.1 %shard_map.95 = (bf16[128,2560]{1,0:T(8,128)(2,1)S(1)}, bf16[2,192,256]{2,1,0:T(8,128)(2,1)S(1)}) custom-call(s32[1]{0:T(128)S(6)} %copy.10.look_hbm, f32[1,192]{1,0:T(1,128)} %bitcast.1, bf16[128,2560]{1,0:T(8,128)(2,1)} %q_hbm.1, bf16[128,2560]{1,0:T(8,128)(2,1)} %k_hbm.1, bf16[128,2560]{1,0:T(8,128)(2,1)} %v_hbm.1, bf16[2560,768]{1,0:T(8,128)(2,1)} %w_hbm.1, ...), custom_call_target="tpu_custom_call" | custom-call | tf_op jit(solution)/shard_map/pallas_call | solution.py:439
  44.4 0.9 %shard_map.96 = (bf16[128,2560]{1,0:T(8,128)(2,1)}, bf16[2,192,256]{2,1,0:T(8,128)(2,1)}) custom-call(bf16[128,2560]{1,0:T(8,128)(2,1)S(1)} %get-tuple-element.4.att_vmem, bf16[2,192,256]{2,1,0:T(8,128)(2,1)S(1)} %get-tuple-element.5.dec_vmem), custom_call_target="tpu_custom_call" | custom-call | tf_op jit(solution)/shard_map/pallas_call | solution.py:474
